TPU v7x, 512 devices: a whole 4x8x8 slice. The times are simulated.
512 devices in a mesh: grp: 8 (over z_lo, x), tile: 64 (over y, z_hi, core).
Axes of the slice: x: 4, y: 8, z: 8 (z_hi: 4, z_lo: 2; z = z_hi * 2 + z_lo), core: 2. Of those that a mesh axis runs over, the one named last changes fastest.
Arguments:
- pixels: bfloat16 [512, 128, 3, 256], P(('grp', 'tile')), parts along dimension 0, may hold values from -6 to 6
- patch_weight: bfloat16 [768, 1024], P('tile'), may hold values from -0.21875 to 0.21875
- qkv_weight: bfloat16 [1024, 1536], P('tile'), may hold values from -2.0625 to 2.0625
- out_weight: bfloat16 [512, 1024], P('tile'), may hold values from -0.25 to 0.25
- reward_head: float32 [1024], replicated, may hold values from -4 to 4
- conv_weight: bfloat16 [3, 3, 48, 3], replicated, may hold values from -1.25 to 1.25
Outputs:
- rewards: float32 [512], P(('grp', 'tile')), parts along dimension 0
- act_grad: bfloat16 [512, 128, 48, 256], P('grp', 'tile'), parts along dimension 0
There are 8 independent parts, one for each index of `grp`. A program takes and returns all parts, laid end to end along the dimension named above; an argument that names none is the same for every part. Nothing has to cross between parts.
All inputs are finite; a program needn't handle non-finite values.
Results may differ from a plain program's by a relative error of at most 0.02.
Values may be sent and summed in bfloat16 or wider, within the bound.
No kernel may reach another device: no remote copies, remote signals or barrier semaphores. Data moves between devices by JAX's collectives and lax.ppermute only.
A program may use at most 64 MiB of HBM per device.

v0:
```python
import jax
import jax.numpy as jnp
from jax import lax
from jax.sharding import PartitionSpec as P

D = 1024
HEADS = 8
HEAD_DIM = 64
PATCH = 16
PDIM = 768
LOSS_SCALE = 1024.0
NORM_EPSILON = 1e-05


def extended(value, sides, width):
    for axis, dim in sides:
        devices, length = (lax.axis_size(axis), value.shape[dim])
        up = [(i, (i + 1) % devices) for i in range(devices - 1)]
        down = [(j, i) for i, j in up]
        last = lax.slice_in_dim(value, length - width, length, axis=dim)
        first = lax.slice_in_dim(value, 0, width, axis=dim)
        before = lax.ppermute(last, axis, up)
        after = lax.ppermute(first, axis, down)
        value = jnp.concatenate([before, value, after], axis=dim)
    return value


def normalize(values_in):
    average = jnp.mean(values_in, -1, keepdims=True)
    centred = values_in - average
    inverse_scale = lax.rsqrt(jnp.mean(centred * centred, -1, keepdims=True) + NORM_EPSILON)
    return (centred * inverse_scale, inverse_scale)


def norm_back(grad_in, normed, inverse_scale):
    return inverse_scale * (
        grad_in
        - jnp.mean(grad_in, -1, keepdims=True)
        - normed * jnp.mean(grad_in * normed, -1, keepdims=True)
    )


def to_patch_rows(pixels):
    frame_count, row_count, _, col_count = pixels.shape
    blocks = pixels.reshape(frame_count, row_count // PATCH, PATCH, 3, col_count // PATCH, PATCH)
    blocks = blocks.transpose(0, 1, 4, 3, 2, 5)
    return blocks.reshape(frame_count, row_count // PATCH * (col_count // PATCH), 3 * PATCH * PATCH)


def from_patch_rows(patches, row_count, col_count):
    frame_count = patches.shape[0]
    blocks = patches.reshape(frame_count, row_count // PATCH, col_count // PATCH, 3, PATCH, PATCH)
    blocks = blocks.transpose(0, 1, 4, 3, 2, 5)
    return blocks.reshape(frame_count, row_count, 3, col_count)


def attend_forward(spread, full_qkv):
    frame_count, local_count, model_width = spread.shape
    score_scale = HEAD_DIM ** (-0.5)
    first_normed, first_scale = normalize(spread.astype(jnp.float32))
    projected = jnp.dot(
        first_normed.astype(jnp.bfloat16).reshape(-1, model_width),
        full_qkv,
        preferred_element_type=jnp.float32,
    )
    projected = projected.astype(jnp.bfloat16).reshape(frame_count, local_count, 3, HEADS, HEAD_DIM)
    query_rows = projected[:, :, 0]
    key_rows = projected[:, :, 1]
    value_rows = projected[:, :, 2]
    scores = (
        jnp.einsum("iphd,jphd->phij", query_rows, key_rows, preferred_element_type=jnp.float32)
        * score_scale
    )
    attn_probs = jax.nn.softmax(scores, axis=-1)
    probs_rounded = attn_probs.astype(jnp.bfloat16)
    attended = jnp.einsum(
        "phij,jphd->iphd", probs_rounded, value_rows, preferred_element_type=jnp.float32
    )
    attended = attended.astype(jnp.bfloat16).reshape(frame_count, local_count, HEADS * HEAD_DIM)
    return (
        first_normed,
        first_scale,
        query_rows,
        key_rows,
        value_rows,
        attn_probs,
        probs_rounded,
        attended,
    )


def attend_backward(grad_spread, saved, back_qkv):
    first_normed, first_scale, query_rows, key_rows, value_rows, attn_probs, probs_rounded, _ = (
        saved
    )
    frame_count, local_count = (first_normed.shape[0], first_normed.shape[1])
    score_scale = HEAD_DIM ** (-0.5)
    grad_heads = grad_spread.reshape(frame_count, local_count, HEADS, HEAD_DIM)
    grad_probs = jnp.einsum(
        "iphd,jphd->phij", grad_heads, value_rows, preferred_element_type=jnp.float32
    )
    grad_value = jnp.einsum(
        "phij,iphd->jphd", probs_rounded, grad_heads, preferred_element_type=jnp.float32
    ).astype(jnp.bfloat16)
    row_delta = jnp.sum(attn_probs * grad_probs, -1, keepdims=True)
    grad_scores = (attn_probs * (grad_probs - row_delta) * score_scale).astype(jnp.bfloat16)
    grad_query = jnp.einsum(
        "phij,jphd->iphd", grad_scores, key_rows, preferred_element_type=jnp.float32
    ).astype(jnp.bfloat16)
    grad_key = jnp.einsum(
        "phij,iphd->jphd", grad_scores, query_rows, preferred_element_type=jnp.float32
    ).astype(jnp.bfloat16)
    grad_proj = jnp.stack([grad_query, grad_key, grad_value], 2).reshape(-1, 3 * HEADS * HEAD_DIM)
    grad_first = jnp.dot(grad_proj, back_qkv.T, preferred_element_type=jnp.float32)
    grad_first = grad_first.reshape(first_normed.shape)
    return norm_back(grad_first, first_normed, first_scale).astype(jnp.bfloat16)


def on_device(pixels, patch_weight, qkv_weight, out_weight, reward_head, conv_weight):
    local_frames, row_count, _, col_count = pixels.shape
    model_width = D
    inner_width = HEADS * HEAD_DIM
    full_patch, full_qkv, full_out = (
        lax.all_gather(patch_weight, "tile", axis=0, tiled=True),
        lax.all_gather(qkv_weight, "tile", axis=0, tiled=True),
        lax.all_gather(out_weight, "tile", axis=0, tiled=True),
    )
    patches = to_patch_rows(pixels)
    patch_count = patches.shape[1]
    spread_patches = lax.all_to_all(patches, "tile", split_axis=1, concat_axis=0, tiled=True)
    frame_count, local_count = (spread_patches.shape[0], spread_patches.shape[1])
    embedded = jnp.dot(
        spread_patches.reshape(-1, PDIM), full_patch, preferred_element_type=jnp.float32
    )
    embedded = embedded.astype(jnp.bfloat16).reshape(frame_count, local_count, model_width)
    saved = attend_forward(embedded, full_qkv)
    hidden = embedded.astype(jnp.float32) + jnp.dot(
        saved[7].reshape(-1, inner_width), full_out, preferred_element_type=jnp.float32
    ).reshape(embedded.shape)
    second_normed, second_scale = normalize(hidden)
    partial_sums = jnp.sum(jnp.sum(second_normed * reward_head, -1), -1)
    all_rewards = lax.psum(partial_sums, "tile") / patch_count
    rewards = lax.dynamic_slice_in_dim(
        all_rewards, lax.axis_index("tile") * local_frames, local_frames
    )
    frame_coeff = -LOSS_SCALE * jax.nn.sigmoid(-all_rewards)
    grad_second = frame_coeff[:, None, None] * reward_head / patch_count
    grad_hidden = norm_back(grad_second, second_normed, second_scale)
    hidden_rounded = grad_hidden.astype(jnp.bfloat16)
    back_patch, back_qkv, back_out = (
        lax.all_gather(patch_weight, "tile", axis=0, tiled=True),
        lax.all_gather(qkv_weight, "tile", axis=0, tiled=True),
        lax.all_gather(out_weight, "tile", axis=0, tiled=True),
    )
    grad_attended = jnp.dot(
        hidden_rounded.reshape(-1, model_width), back_out.T, preferred_element_type=jnp.float32
    )
    grad_attended = grad_attended.astype(jnp.bfloat16).reshape(
        hidden.shape[0], hidden.shape[1], inner_width
    )
    grad_embed = attend_backward(grad_attended, saved, back_qkv)
    grad_total = (grad_hidden + grad_embed.astype(jnp.float32)).astype(jnp.bfloat16)
    grad_patches = jnp.dot(
        grad_total.reshape(-1, model_width), back_patch.T, preferred_element_type=jnp.float32
    )
    grad_patches = grad_patches.astype(jnp.bfloat16).reshape(hidden.shape[0], hidden.shape[1], PDIM)
    home_patches = lax.all_to_all(grad_patches, "tile", split_axis=0, concat_axis=1, tiled=True)
    grad_pixels = from_patch_rows(home_patches, row_count, col_count)
    row_grad = lax.all_to_all(grad_pixels, "tile", split_axis=1, concat_axis=0, tiled=True)
    tile_rows = row_grad.shape[1]
    padded = extended(row_grad, (("tile", 1),), 1)
    padded = jnp.pad(padded, ((0, 0), (0, 0), (0, 0), (1, 1)))
    pieces = [
        padded[:, 2 - row_off : 2 - row_off + tile_rows, :, 2 - col_off : 2 - col_off + col_count]
        for row_off in range(3)
        for col_off in range(3)
    ]
    stacked = jnp.stack(pieces, 2).reshape(row_grad.shape[0], tile_rows, 27, col_count)
    kernel = conv_weight.transpose(0, 1, 3, 2).reshape(27, -1)
    act_grad = jnp.einsum(
        "fykx,kc->fycx", stacked, kernel, preferred_element_type=jnp.float32
    ).astype(jnp.bfloat16)
    return (rewards, act_grad)


def solution(mesh):
    in_specs = (
        P(("grp", "tile"), None, None, None),
        P("tile", None),
        P("tile", None),
        P("tile", None),
        P(),
        P(),
    )
    out_specs = (P(("grp", "tile")), P("grp", "tile", None, None))
    return jax.shard_map(
        on_device, mesh=mesh, in_specs=in_specs, out_specs=out_specs, check_vma=False
    )
```

profile of v0, /device:TPU:1, one launch (start us, length us, event | category | flops | bytes accessed | tf_op | source)
XLA Modules:
  0.0 508.4 jit_solution(12765785373744496446)
XLA Ops:
  7.2 0.7 all-gather.9.cloned.1.call-update
  7.9 0.7 all-gather.5.cloned.1.call-update
  8.6 2.1 reshape.213
  11.2 1.1 reshape.230
  12.3 0.5 broadcast.207
  12.8 1.8 reduce.4
  14.6 0.8 reshape.233
  15.3 17.6 %all-to-all-start = ((bf16[64,2,768]{2,1,0:T(2,128)(2,1)}), bf16[64,2,768]{2,1,0:T(2,128)(2,1)S(1)}, u32[]{:S(2)}, u32[]{:S(2)}) async-start(bf16[64,2,768]{2,1,0:T(2,128)(2,1)} %reshape.233), calls=%async_computation | async-start | bytes 393216 | tf_op jit(solution)/shard_map/all_to_all | solution.py:130
  33.0 0.7 all-gather.7.cloned.1.call-update
  33.7 14.1 %all-to-all-done = bf16[64,2,768]{2,1,0:T(2,128)(2,1)S(1)} async-done(((bf16[64,2,768]{2,1,0:T(2,128)(2,1)}), bf16[64,2,768]{2,1,0:T(2,128)(2,1)S(1)}, u32[]{:S(2)}, u32[]{:S(2)}) %all-to-all-start) | async-done | bytes 196640 | tf_op jit(solution)/shard_map/all_to_all | solution.py:130
  47.9 55.3 %all-gather.9.cloned.1.call-done = bf16[64,12,1024]{2,1,0:T(8,128)(2,1)} async-done(((bf16[1,12,1024]{2,1,0:T(8,128)(2,1)}), bf16[64,12,1024]{2,1,0:T(8,128)(2,1)}) %all-gather.9.cloned.1.call-update) | async-done | bytes 1572880 | tf_op jit(solution)/shard_map/all_gather | solution.py:124
  103.2 2.5 reshape.226
  105.7 0.5 fusion.53
  107.0 0.7 copy.178
  107.7 81.3 %all-gather.5.cloned.1.call-done = bf16[1024,1536]{1,0:T(8,128)(2,1)} async-done(((bf16[16,1536]{1,0:T(8,128)(2,1)}), bf16[1024,1536]{1,0:T(8,128)(2,1)}) %all-gather.5.cloned.1.call-update) | async-done | bytes 3145744 | tf_op jit(solution)/shard_map/all_gather | solution.py:125
  189.0 2.5 convolution_convert_fusion
  191.6 0.4 reshape.216
  192.0 0.9 fusion.51
  193.2 1.4 fusion.54
  194.6 0.6 copy-done.10
  195.4 76.6 %all-gather.7.cloned.1.call-done = bf16[512,1024]{1,0:T(8,128)(2,1)} async-done(((bf16[8,1024]{1,0:T(8,128)(2,1)}), bf16[512,1024]{1,0:T(8,128)(2,1)}) %all-gather.7.cloned.1.call-update) | async-done | bytes 1048592 | tf_op jit(solution)/shard_map/all_gather | solution.py:126
  272.0 1.7 fusion.55
  274.2 138.3 %psum.7 = f32[64]{0:T(128)S(1)} all-reduce(f32[64]{0:T(128)S(1)} %multiply_reduce_fusion.3), channel_id=1, replica_groups=mesh['grp'=8,'tile'=64] {'tile'}, use_global_device_ids=true, to_apply=%region_7.0 | all-reduce | flops 64 | bytes 512 | tf_op jit(solution)/shard_map/psum | solution.py:142
  412.4 0.5 divide_multiply_fusion
  413.5 0.5 copy-done
  414.6 1.7 convolution_convert_fusion.7
  416.8 1.1 fusion.22
  417.9 2.7 fusion.13
  420.6 2.6 fusion.14
  423.1 1.4 fusion.15
  424.8 1.3 copy.177
  426.0 1.8 dot_general.54
  427.8 3.2 fusion.50
  431.8 0.7 convolution_convert_fusion.6
  432.6 23.5 %all_to_all.30 = bf16[64,2,768]{2,1,0:T(2,128)(2,1)S(1)} all-to-all(bf16[64,2,768]{2,1,0:T(2,128)(2,1)S(1)} %reshape.219), channel_id=1, replica_groups=mesh['grp'=8,'tile'=64] {'tile'}, dimensions={0} | all-to-all | bytes 393216 | tf_op jit(solution)/shard_map/all_to_all | solution.py:167
  456.1 1.1 reshape.220
  457.6 1.8 reshape.231
  459.4 19.2 %all_to_all.31 = bf16[1,128,3,256]{3,2,0,1:T(4,128)(2,1)S(1)} all-to-all(bf16[1,128,3,256]{3,2,0,1:T(4,128)(2,1)S(1)} %reshape.231), channel_id=1, replica_groups=mesh['grp'=8,'tile'=64] {'tile'}, dimensions={1} | all-to-all | bytes 393216 | tf_op jit(solution)/shard_map/all_to_all | solution.py:169
  479.1 3.3 collective-permute-start
  482.4 2.1 collective-permute-start.1
  484.6 0.6 dynamic_slice.3
  485.2 8.7 %collective-permute-done.1 = bf16[64,1,3,256]{3,1,0,2:T(2,128)(2,1)S(1)} collective-permute-done((bf16[64,1,3,256]{3,1,0,2:T(2,128)(2,1)S(1)}, bf16[64,1,3,256]{3,1,0,2:T(2,128)(2,1)S(1)}, u32[]{:S(2)}, u32[]{:S(2)}) %collective-permute-start.1) | collective-permute-done | bytes 98336 | tf_op jit(solution)/shard_map/ppermute | solution.py:23
  493.8 1.8 select_maximum_fusion
  495.6 0.5 fusion.38
  496.1 0.5 fusion.37
  496.9 0.5 fusion.34
  498.2 0.4 fusion.31
  498.8 3.1 convert_bitcast_fusion
  (66 shorter events, 7.3 us)
Async XLA Ops:
  7.2 96.0 %all-gather.9.cloned.1.call-start = ((), (), s32[]{:S(2)}) async-start(), calls=%async_computation.5 | async-start | bytes 2129920 | tf_op jit(solution)/shard_map/all_gather | solution.py:124
  7.9 181.1 %all-gather.5.cloned.1.call-start = ((), (), s32[]{:S(2)}) async-start(), calls=%async_computation.3 | async-start | bytes 3194880 | tf_op jit(solution)/shard_map/all_gather | solution.py:125
  15.3 32.4 %all-to-all-start = ((bf16[64,2,768]{2,1,0:T(2,128)(2,1)}), bf16[64,2,768]{2,1,0:T(2,128)(2,1)S(1)}, u32[]{:S(2)}, u32[]{:S(2)}) async-start(bf16[64,2,768]{2,1,0:T(2,128)(2,1)} %reshape.233), calls=%async_computation | async-start | bytes 393216 | tf_op jit(solution)/shard_map/all_to_all | solution.py:130
  32.9 239.1 %all-gather.7.cloned.1.call-start = ((), (), s32[]{:S(2)}) async-start(), calls=%async_computation.4 | async-start | bytes 1064960 | tf_op jit(solution)/shard_map/all_gather | solution.py:126
  194.6 0.6 copy-start.10
  194.6 77.4 %copy-start.9 = (f32[2,8,64,64]{2,3,1,0:T(8,128)}, f32[2,8,64,64]{2,3,1,0:T(8,128)S(1)}, u32[]{:S(2)}) copy-start(f32[2,8,64,64]{2,3,1,0:T(8,128)S(1)} %get-tuple-element.16) | copy-start | bytes 786436
  195.4 78.5 %copy-start.5 = (f32[1024]{0:T(1024)S(1)}, f32[1024]{0:T(1024)}, u32[]{:S(2)}) copy-start(f32[1024]{0:T(1024)} %param.10) | copy-start | bytes 12292
  413.3 0.7 copy-start
  416.8 3.7 copy-start.2
  416.8 3.7 copy-start.11
  423.1 1.4 copy-start.3
  423.1 1.4 copy-start.4
  424.7 3.0 copy-start.7
  427.8 3.2 copy-start.1
  457.6 26.9 %copy-start.6 = (bf16[3,3,48,3]{2,3,1,0:T(4,128)(2,1)S(1)}, bf16[3,3,48,3]{2,3,1,0:T(4,128)(2,1)}, u32[]{:S(2)}) copy-start(bf16[3,3,48,3]{2,3,1,0:T(4,128)(2,1)} %param.11) | copy-start | bytes 7780
  457.6 26.9 %copy-start.8 = (f32[64]{0:T(128)S(1)}, f32[64]{0:T(128)}, u32[]{:S(2)}) copy-start(f32[64]{0:T(128)} %get-tuple-element.12) | copy-start | bytes 772
  479.1 6.1 %collective-permute-start = (bf16[64,1,3,256]{3,1,0,2:T(2,128)(2,1)S(1)}, bf16[64,1,3,256]{3,1,0,2:T(2,128)(2,1)S(1)}, u32[]{:S(2)}, u32[]{:S(2)}) collective-permute-start(bf16[64,1,3,256]{3,1,0,2:T(2,128)(2,1)S(1)} %get-tuple-element.7), channel_id=1, source_target_pairs={{0,1},{1,2},{2,3},{3,4},{4,5},{5,6},{6,7},{7,8},{8,9},{9,10},{10,1... | collective-permute-start | bytes 294920 | tf_op jit(solution)/shard_map/ppermute | solution.py:22
  482.4 11.5 %collective-permute-start.1 = (bf16[64,1,3,256]{3,1,0,2:T(2,128)(2,1)S(1)}, bf16[64,1,3,256]{3,1,0,2:T(2,128)(2,1)S(1)}, u32[]{:S(2)}, u32[]{:S(2)}) collective-permute-start(bf16[64,1,3,256]{3,1,0,2:T(2,128)(2,1)S(1)} %get-tuple-element.8), channel_id=1, source_target_pairs={{1,0},{2,1},{3,2},{4,3},{5,4},{6,5},{7,6},{8,7},{9,8},{10,9},{11,1... | collective-permute-start | bytes 294920 | tf_op jit(solution)/shard_map/ppermute | solution.py:23
Sparse Core Ops, SparseCore 0:
  11.3 91.8 all-gather.8
  106.5 82.4 all-gather.4
  192.3 79.6 all-gather.6
where the time goes:
time: 509 us; the launch traced here: 508 us
  waiting for transfers between devices  238 us (47%)
  blocking collectives  181 us (36%)
  starting transfers between devices  23.1 us (5%)
  matrix products  22.6 us (4%)
  local copies, waits for them, and re-layouts  22.4 us (4%)
  between operations  14.2 us (3%)
  other arithmetic  7.14 us (1%)
    psum x1, blocking collectives, on_device(): all_rewards = lax.psum(partial_sums, 'tile') / patch_count  138 us
    all_gather x1, waiting for transfers between devices, on_device(): lax.all_gather(qkv_weight, 'tile', axis=0, tiled=True)  81.3 us
    all_gather x1, waiting for transfers between devices, on_device(): lax.all_gather(out_weight, 'tile', axis=0, tiled=True)  76.6 us
    all_gather x1, waiting for transfers between devices, on_device(): lax.all_gather(patch_weight, 'tile', axis=0, tiled=True)  55.3 us
    all_to_all x1, blocking collectives, on_device(): lax.all_to_all(grad_patches, 'tile', split_axis=0, concat_axis=1, tiled=T...  23.5 us
    all_to_all x1, blocking collectives, on_device(): lax.all_to_all(grad_pixels, 'tile', split_axis=1, concat_axis=0, tiled=True)  19.2 us
    all_to_all x1, starting transfers between devices, on_device(): lax.all_to_all(patches, 'tile', split_axis=1, concat_axis=0, tiled=True)  17.6 us
    all_to_all x1, waiting for transfers between devices, on_device(): lax.all_to_all(patches, 'tile', split_axis=1, concat_axis=0, tiled=True)  14.1 us
  transfers between devices with their start and end apart: 6, of which 5 were waited for; matrix products, arithmetic and copies ran while one was open for 3% of the time, Pallas kernels for 0%

commit v1 on v0

--- a/solution.py
+++ b/solution.py
@@ -10,6 +10,10 @@
 PDIM = 768
 LOSS_SCALE = 1024.0
 NORM_EPSILON = 1e-05
+
+
+def loops_pair(vals):
+    return jnp.sum(lax.all_gather(vals, "tile"), 0)
 
 
 def extended(value, sides, width):
@@ -139,7 +143,7 @@
     ).reshape(embedded.shape)
     second_normed, second_scale = normalize(hidden)
     partial_sums = jnp.sum(jnp.sum(second_normed * reward_head, -1), -1)
-    all_rewards = lax.psum(partial_sums, "tile") / patch_count
+    all_rewards = loops_pair(partial_sums) / patch_count
     rewards = lax.dynamic_slice_in_dim(
         all_rewards, lax.axis_index("tile") * local_frames, local_frames
     )

time: 509 us -> 646 us (1.27)
  blocking collectives: 181 us -> 317 us
    unnamed x0 -> x1, blocking collectives: none -> 272 us
    psum x1 -> x0, blocking collectives: 138 us -> none  [on_device(): all_rewards = lax.psum(partial_sums, 'tile') / patch_count]
where the time goes in v1:
time: 646 us; the launch traced here: 645 us
  blocking collectives  317 us (49%)
  waiting for transfers between devices  236 us (37%)
  local copies, waits for them, and re-layouts  24 us (4%)
  starting transfers between devices  23.1 us (4%)
  matrix products  22.6 us (3%)
  between operations  14.9 us (2%)
  other arithmetic  7.17 us (1%)
    unnamed x1, blocking collectives  272 us
    all_gather x1, waiting for transfers between devices, on_device(): lax.all_gather(qkv_weight, 'tile', axis=0, tiled=True)  81.3 us
    all_gather x1, waiting for transfers between devices, on_device(): lax.all_gather(out_weight, 'tile', axis=0, tiled=True)  76.6 us
    all_gather x1, waiting for transfers between devices, on_device(): lax.all_gather(patch_weight, 'tile', axis=0, tiled=True)  55.3 us
    all_to_all x1, blocking collectives, on_device(): lax.all_to_all(grad_patches, 'tile', split_axis=0, concat_axis=1, tiled=T...  26 us
    all_to_all x1, blocking collectives, on_device(): lax.all_to_all(grad_pixels, 'tile', split_axis=1, concat_axis=0, tiled=True)  19.2 us
    all_to_all x1, starting transfers between devices, on_device(): lax.all_to_all(patches, 'tile', split_axis=1, concat_axis=0, tiled=True)  17.6 us
  transfers between devices with their start and end apart: 6, of which 5 were waited for; matrix products, arithmetic and copies ran while one was open for 3% of the time, Pallas kernels for 0%

profile of v1, /device:TPU:1, one launch (start us, length us, event | category | flops | bytes accessed | tf_op | source)
XLA Modules:
  0.0 645.3 jit_solution(7740311417812628561)
XLA Ops:
  7.2 0.7 all-gather.10.cloned.1.call-update
  7.9 0.7 all-gather.6.cloned.1.call-update
  8.6 2.1 reshape.224
  11.2 1.1 reshape.247
  12.3 0.5 broadcast.224
  12.8 1.8 reduce.4
  14.6 0.8 reshape.250
  15.3 17.6 %all-to-all-start = ((bf16[64,2,768]{2,1,0:T(2,128)(2,1)}), bf16[64,2,768]{2,1,0:T(2,128)(2,1)S(1)}, u32[]{:S(2)}, u32[]{:S(2)}) async-start(bf16[64,2,768]{2,1,0:T(2,128)(2,1)} %reshape.250), calls=%async_computation | async-start | bytes 393216 | tf_op jit(solution)/shard_map/all_to_all | solution.py:134
  33.0 0.7 all-gather.8.cloned.1.call-update
  33.7 1.3 dynamic-slice
  35.6 12.1 %all-to-all-done = bf16[64,2,768]{2,1,0:T(2,128)(2,1)S(1)} async-done(((bf16[64,2,768]{2,1,0:T(2,128)(2,1)}), bf16[64,2,768]{2,1,0:T(2,128)(2,1)S(1)}, u32[]{:S(2)}, u32[]{:S(2)}) %all-to-all-start) | async-done | bytes 196640 | tf_op jit(solution)/shard_map/all_to_all | solution.py:134
  47.9 55.3 %all-gather.10.cloned.1.call-done = bf16[64,12,1024]{2,1,0:T(8,128)(2,1)} async-done(((bf16[1,12,1024]{2,1,0:T(8,128)(2,1)}), bf16[64,12,1024]{2,1,0:T(8,128)(2,1)}) %all-gather.10.cloned.1.call-update) | async-done | bytes 1572880 | tf_op jit(solution)/shard_map/all_gather | solution.py:128
  103.2 2.5 reshape.241
  105.7 0.5 fusion.53
  107.0 0.7 copy.178
  107.7 81.3 %all-gather.6.cloned.1.call-done = bf16[1024,1536]{1,0:T(8,128)(2,1)} async-done(((bf16[16,1536]{1,0:T(8,128)(2,1)}), bf16[1024,1536]{1,0:T(8,128)(2,1)}) %all-gather.6.cloned.1.call-update) | async-done | bytes 3145744 | tf_op jit(solution)/shard_map/all_gather | solution.py:129
  189.0 2.5 convolution_convert_fusion
  191.6 0.4 reshape.227
  192.0 0.9 fusion.51
  193.2 1.4 fusion.54
  194.6 0.6 copy-done.10
  195.4 76.6 %all-gather.8.cloned.1.call-done = bf16[512,1024]{1,0:T(8,128)(2,1)} async-done(((bf16[8,1024]{1,0:T(8,128)(2,1)}), bf16[512,1024]{1,0:T(8,128)(2,1)}) %all-gather.8.cloned.1.call-update) | async-done | bytes 1048592 | tf_op jit(solution)/shard_map/all_gather | solution.py:130
  272.0 1.7 fusion.55
  274.5 272.2 %all-reduce.1 = f32[4096]{0:T(1024)S(1)} all-reduce(f32[4096]{0:T(1024)S(1)} %dynamic-update-slice), channel_id=2, replica_groups=mesh['grp'=8,'tile'=64] {'tile'}, use_global_device_ids=true, to_apply=%add.1 | all-reduce | flops 4096 | bytes 32768
  546.8 0.5 divide_multiply_fusion
  547.9 0.5 copy-done
  548.9 1.7 convolution_convert_fusion.7
  551.2 1.1 fusion.22
  552.2 2.7 fusion.13
  554.9 2.6 fusion.14
  557.5 1.4 fusion.15
  559.1 1.3 copy.177
  560.4 1.8 dot_general.54
  562.1 3.2 fusion.50
  566.2 0.7 convolution_convert_fusion.6
  566.9 26.0 %all_to_all.30 = bf16[64,2,768]{2,1,0:T(2,128)(2,1)S(1)} all-to-all(bf16[64,2,768]{2,1,0:T(2,128)(2,1)S(1)} %reshape.230), channel_id=1, replica_groups=mesh['grp'=8,'tile'=64] {'tile'}, dimensions={0} | all-to-all | bytes 393216 | tf_op jit(solution)/shard_map/all_to_all | solution.py:171
  593.0 1.1 reshape.231
  594.5 1.8 reshape.248
  596.3 19.2 %all_to_all.31 = bf16[1,128,3,256]{3,2,0,1:T(4,128)(2,1)S(1)} all-to-all(bf16[1,128,3,256]{3,2,0,1:T(4,128)(2,1)S(1)} %reshape.248), channel_id=1, replica_groups=mesh['grp'=8,'tile'=64] {'tile'}, dimensions={1} | all-to-all | bytes 393216 | tf_op jit(solution)/shard_map/all_to_all | solution.py:173
  616.0 3.3 collective-permute-start
  619.3 2.1 collective-permute-start.1
  621.5 0.6 dynamic_slice.3
  622.0 8.7 %collective-permute-done.1 = bf16[64,1,3,256]{3,1,0,2:T(2,128)(2,1)S(1)} collective-permute-done((bf16[64,1,3,256]{3,1,0,2:T(2,128)(2,1)S(1)}, bf16[64,1,3,256]{3,1,0,2:T(2,128)(2,1)S(1)}, u32[]{:S(2)}, u32[]{:S(2)}) %collective-permute-start.1) | collective-permute-done | bytes 98336 | tf_op jit(solution)/shard_map/ppermute | solution.py:27
  630.7 1.8 select_maximum_fusion
  632.5 0.5 fusion.38
  633.0 0.5 fusion.37
  633.8 0.5 fusion.34
  635.7 3.1 convert_bitcast_fusion
  (71 shorter events, 8.1 us)
Async XLA Ops:
  7.2 96.0 %all-gather.10.cloned.1.call-start = ((), (), s32[]{:S(2)}) async-start(), calls=%async_computation.5 | async-start | bytes 2129920 | tf_op jit(solution)/shard_map/all_gather | solution.py:128
  7.9 181.1 %all-gather.6.cloned.1.call-start = ((), (), s32[]{:S(2)}) async-start(), calls=%async_computation.3 | async-start | bytes 3194880 | tf_op jit(solution)/shard_map/all_gather | solution.py:129
  15.3 32.4 %all-to-all-start = ((bf16[64,2,768]{2,1,0:T(2,128)(2,1)}), bf16[64,2,768]{2,1,0:T(2,128)(2,1)S(1)}, u32[]{:S(2)}, u32[]{:S(2)}) async-start(bf16[64,2,768]{2,1,0:T(2,128)(2,1)} %reshape.250), calls=%async_computation | async-start | bytes 393216 | tf_op jit(solution)/shard_map/all_to_all | solution.py:134
  32.9 239.1 %all-gather.8.cloned.1.call-start = ((), (), s32[]{:S(2)}) async-start(), calls=%async_computation.4 | async-start | bytes 1064960 | tf_op jit(solution)/shard_map/all_gather | solution.py:130
  194.6 0.6 copy-start.10
  194.6 77.4 %copy-start.9 = (f32[2,8,64,64]{2,3,1,0:T(8,128)}, f32[2,8,64,64]{2,3,1,0:T(8,128)S(1)}, u32[]{:S(2)}) copy-start(f32[2,8,64,64]{2,3,1,0:T(8,128)S(1)} %get-tuple-element.16) | copy-start | bytes 786436
  195.4 78.5 %copy-start.5 = (f32[1024]{0:T(1024)S(1)}, f32[1024]{0:T(1024)}, u32[]{:S(2)}) copy-start(f32[1024]{0:T(1024)} %param.10) | copy-start | bytes 12292
  547.6 0.7 copy-start
  551.1 3.7 copy-start.2
  551.2 3.7 copy-start.11
  557.5 1.4 copy-start.3
  557.5 1.4 copy-start.4
  559.1 3.0 copy-start.7
  562.1 3.2 copy-start.1
  594.5 26.9 %copy-start.6 = (bf16[3,3,48,3]{2,3,1,0:T(4,128)(2,1)S(1)}, bf16[3,3,48,3]{2,3,1,0:T(4,128)(2,1)}, u32[]{:S(2)}) copy-start(bf16[3,3,48,3]{2,3,1,0:T(4,128)(2,1)} %param.11) | copy-start | bytes 7780
  594.5 26.9 %copy-start.8 = (f32[64]{0:T(128)S(1)}, f32[64]{0:T(128)}, u32[]{:S(2)}) copy-start(f32[64]{0:T(128)} %get-tuple-element.12) | copy-start | bytes 772
  616.0 6.1 collective-permute-start
  619.3 11.5 %collective-permute-start.1 = (bf16[64,1,3,256]{3,1,0,2:T(2,128)(2,1)S(1)}, bf16[64,1,3,256]{3,1,0,2:T(2,128)(2,1)S(1)}, u32[]{:S(2)}, u32[]{:S(2)}) collective-permute-start(bf16[64,1,3,256]{3,1,0,2:T(2,128)(2,1)S(1)} %get-tuple-element.8), channel_id=1, source_target_pairs={{1,0},{2,1},{3,2},{4,3},{5,4},{6,5},{7,6},{8,7},{9,8},{10,9},{11,1... | collective-permute-start | bytes 294920 | tf_op jit(solution)/shard_map/ppermute | solution.py:27
Sparse Core Ops, SparseCore 0:
  11.3 91.8 all-gather.9
  106.5 82.4 all-gather.5
  192.3 79.6 all-gather.7
